TPU v7x, 128 devices: a whole 4x4x4 slice. The times are simulated.
128 devices in a mesh: sub: 16 (over x, y), row: 8 (over z, core).
Axes of the slice: x: 4, y: 4, z: 4, core: 2. Of those that a mesh axis runs over, the one named last changes fastest.
Arguments:
- sigma_top: float32 [6144, 6144], P('row', 'sub'), may hold values from -2 to 4, as said below
- coupling: float32 [16, 6144, 768], P('sub', 'row'), may hold values from -0.16 to 0.16
- child_inverse: float32 [16, 768, 768], P('sub', 'row'), may hold values from -1 to 10, as said below
- tile_mask: int32 [16, 24], P('sub'), may hold values 0 or 1
- obs_node: int32 [32768], P(('sub', 'row')), may hold values from 0 to 12287
- obs_noise: float32 [32768], P(('sub', 'row')), may hold values from 0.05 to 2
Outputs:
- sep_child: float32 [16, 6144, 768], P('sub', 'row')
- child_block: float32 [16, 768, 768], P('sub', 'row')
- loo_var: float32 [32768], P(('sub', 'row'))
Inputs may be any that keep to these rules, and one draw needn't show every extreme that they name: sigma_top is exactly symmetric. Each child_inverse[c] is exactly symmetric.
All inputs are finite; a program needn't handle non-finite values. No bound on the sum of `tile_mask` on one device may be relied on, other than what follows from the above.
Results may differ from a plain program's by a relative error of at most 0.000073.
Values sent between devices are 32-bit elements; how exact they have to be, the bound alone decides.
No kernel may reach another device: no remote copies, remote signals or barrier semaphores. Data moves between devices by JAX's collectives and lax.ppermute only.
A program may use at most 128 MiB of HBM per device.

v0:
```python
import jax
import jax.numpy as jnp
from jax import lax
from jax.sharding import PartitionSpec as P

TILE = 256


def local(sigma_top, coupling, child_inverse, tile_mask, obs_node, obs_noise):
    highest = lax.Precision.HIGHEST
    rows_here = coupling.shape[1]
    width_here = child_inverse.shape[1]
    tiles_here = rows_here // TILE
    row_index = lax.axis_index("row")
    mask_here = lax.dynamic_slice_in_dim(tile_mask[0], row_index * tiles_here, tiles_here)
    row_mask = jnp.repeat(mask_here, TILE).astype(jnp.float32)
    masked = coupling[0] * row_mask[:, None]
    gathered = lax.all_gather(masked, "row", axis=0, tiled=True)
    product = jnp.dot(
        lax.all_gather(sigma_top, "sub", axis=1, tiled=True),
        gathered,
        precision=highest,
        preferred_element_type=jnp.float32,
    )
    sep_part = -product
    update = lax.psum_scatter(
        lax.dot_general(
            masked,
            sep_part,
            (((0,), (0,)), ((), ())),
            precision=highest,
            preferred_element_type=jnp.float32,
        ),
        "row",
        scatter_dimension=0,
        tiled=True,
    )
    block_here = child_inverse[0] - update
    own_cols = lax.dynamic_slice_in_dim(block_here, row_index * width_here, width_here, 1)
    own_diag = jnp.diagonal(own_cols)
    every_var = lax.all_gather(own_diag, ("sub", "row"), axis=0, tiled=True)
    loo_var = every_var[obs_node] + obs_noise
    return (sep_part[None], block_here[None], loo_var)


def solution(mesh):
    placed = (
        P("row", "sub"),
        P("sub", "row", None),
        P("sub", "row", None),
        P("sub", None),
        P(("sub", "row")),
        P(("sub", "row")),
    )
    return jax.shard_map(
        local,
        mesh=mesh,
        in_specs=placed,
        out_specs=(P("sub", "row", None), P("sub", "row", None), P(("sub", "row"))),
        check_vma=False,
    )
```

profile of v0, /device:TPU:1, one launch (start us, length us, event | category | flops | bytes accessed | tf_op | source)
XLA Modules:
  0.0 450.1 jit_solution(1674996634150140336)
XLA Ops:
  7.2 0.0 all-gather.3.cloned.1.call-start
  7.2 0.7 convert_bitcast_fusion
  7.9 0.1 broadcast_in_dim.17
  8.0 3.3 bitcast_multiply_fusion
  11.3 0.0 all-gather.5.cloned.1.call-start
  11.4 0.7 all-gather.5.cloned.1.call-update
  12.1 0.0 reduce-scatter.2.cloned.1.call-start
  12.2 97.0 %all-gather.3.cloned.1.call-done = f32[6144,768]{1,0:T(8,128)} async-done(((f32[768,768]{1,0:T(8,128)}), f32[6144,768]{1,0:T(8,128)}) %all-gather.3.cloned.1.call-update) | async-done | bytes 18874384 | tf_op jit(solution)/shard_map/all_gather | solution.py:18
  109.1 124.2 %all-gather.5.cloned.1.call-done = f32[768,6144]{1,0:T(8,128)} async-done(((f32[768,384]{1,0:T(8,128)}), f32[768,6144]{1,0:T(8,128)}) %all-gather.5.cloned.1.call-update) | async-done | bytes 18874384 | tf_op jit(solution)/shard_map/all_gather | solution.py:20
  233.4 92.2 %fusion.2 = f32[768,768]{1,0:T(8,128)S(1)} fusion(f32[6144,768]{1,0:T(8,128)} %all-gather.3.cloned.1.call-done, f32[768,6144]{1,0:T(8,128)} %all-gather.5.cloned.1.call-done), kind=kOutput, calls=%fused_computation.12 | convolution fusion | flops 43486543872 | bytes 40108032 | tf_op jit(solution)/shard_map/dot_general | solution.py:19
  325.5 1.4 copy-done.1
  326.9 12.5 %fusion = f32[768,768]{1,0:T(8,128)} fusion(f32[768,768]{1,0:T(8,128)S(1)} %copy-done, f32[768,768]{1,0:T(8,128)S(1)} %fusion.2), kind=kOutput, calls=%fused_computation.3 | convolution fusion | flops 5436407808 | bytes 7077888 | tf_op jit(solution)/shard_map/dot_general | solution.py:27
  339.5 0.6 copy-done.6
  340.2 1.0 copy-done.2
  341.2 1.6 negate_bitcast_fusion
  342.7 3.1 copy.10
  345.8 24.8 %reduce-scatter.2.cloned.1.call-done = f32[96,768]{1,0:T(8,128)} async-done(((f32[768,768]{1,0:T(8,128)}), f32[96,768]{1,0:T(8,128)}) %reduce-scatter.2.cloned.1.call-update) | async-done | bytes 294928 | tf_op jit(solution)/shard_map/reduce_scatter | solution.py:26
  370.6 1.0 bitcast_subtract_fusion
  371.6 0.1 constant_dynamic-slice_fusion
  371.7 1.2 gather_fusion
  373.0 0.3 dynamic-update-slice
  373.2 68.1 %all-reduce = f32[12288]{0:T(1024)S(1)} all-reduce(f32[12288]{0:T(1024)S(1)} %dynamic-update-slice), channel_id=1, replica_groups=mesh['sub'=16,'row'=8] {'sub','row'}, use_global_device_ids=true, to_apply=%add | all-reduce | flops 12288 | bytes 98304
  441.3 1.7 gather_fusion.1
  443.1 0.6 add.25
  (18 shorter events, 0.1 us)
Async XLA Ops:
  7.2 102.0 %all-gather.3.cloned.1.call-start = ((), (), s32[]{:S(2)}) async-start(), calls=%async_computation.1 | async-start | bytes 21233664 | tf_op jit(solution)/shard_map/all_gather | solution.py:18
  11.3 222.0 %all-gather.5.cloned.1.call-start = ((), (), s32[]{:S(2)}) async-start(), calls=%async_computation.2 | async-start | bytes 20054016 | tf_op jit(solution)/shard_map/all_gather | solution.py:20
  12.1 314.8 %copy-start = (f32[768,768]{1,0:T(8,128)S(1)}, f32[768,768]{1,0:T(8,128)}, u32[]{:S(2)}) copy-start(f32[768,768]{1,0:T(8,128)} %bitcast_multiply_fusion) | copy-start | bytes 7077892
  12.1 358.5 %reduce-scatter.2.cloned.1.call-start = ((), (), s32[]{:S(2)}) async-start(), calls=%async_computation.3 | async-start | bytes 2654208 | tf_op jit(solution)/shard_map/reduce_scatter | solution.py:26
  325.5 1.4 copy-start.1
  339.5 0.7 copy-start.6
  339.5 1.7 copy-start.2
  342.7 27.9 %copy-start.4 = (f32[1,96,768]{2,1,0:T(8,128)S(1)}, f32[1,96,768]{2,1,0:T(8,128)}, u32[]{:S(2)}) copy-start(f32[1,96,768]{2,1,0:T(8,128)} %param.8) | copy-start | bytes 884740
  345.8 97.2 %copy-start.5 = (f32[256]{0:T(256)S(1)}, f32[256]{0:T(256)}, u32[]{:S(2)}) copy-start(f32[256]{0:T(256)} %param.11) | copy-start | bytes 3076
  371.6 72.0 %copy-start.3 = (f32[96,768]{1,0:T(8,128)}, f32[96,768]{1,0:T(8,128)S(1)}, u32[]{:S(2)}) copy-start(f32[96,768]{1,0:T(8,128)S(1)} %bitcast_subtract_fusion) | copy-start | bytes 884740
Sparse Core Ops, SparseCore 0:
  11.5 97.6 all-gather.2
  111.3 121.9 all-gather.4
  339.6 30.9 reduce-scatter.1
where the time goes:
time: 450 us
  waiting for transfers between devices  247 us (55%)
  matrix products  105 us (23%)
  blocking collectives  68.1 us (15%)
  between operations  13.8 us (3%)
  local copies, waits for them, and re-layouts  9.55 us (2%)
  other arithmetic  7.17 us (2%)
    all_gather x1, waiting for transfers between devices, local(): lax.all_gather(sigma_top, 'sub', axis=1, tiled=True)  124 us
    all_gather x1, waiting for transfers between devices, local(): gathered = lax.all_gather(masked, 'row', axis=0, tiled=True)  97 us
    dot_general x1, matrix products, local(): jnp.dot(lax.all_gather(sigma_top, 'sub', axis=1, tiled=True), gathered, p...  92.2 us
    unnamed x1, blocking collectives  68.1 us
    reduce_scatter x1, waiting for transfers between devices, local(): lax.psum_scatter(lax.dot_general(masked, sep_part, (((0,), (0,)), ((), ()...  24.8 us
    dot_general x1, matrix products, local(): lax.dot_general(masked, sep_part, (((0,), (0,)), ((), ())), precision=hig...  12.5 us
  transfers between devices with their start and end apart: 3, of which 3 were waited for; matrix products, arithmetic and copies ran while one was open for 1% of the time, Pallas kernels for 0%

commit v1 on v0

--- a/solution.py
+++ b/solution.py
@@ -7,6 +7,13 @@
 
 
 def local(sigma_top, coupling, child_inverse, tile_mask, obs_node, obs_noise):
+
+    def pass_the_spots(local_x, axis_no):
+        return jnp.concatenate(
+            jax.lax.all_to_all(jnp.stack(jax.lax.axis_size("sub") * [local_x]), "sub", 0, 0),
+            axis_no,
+        )
+
     highest = lax.Precision.HIGHEST
     rows_here = coupling.shape[1]
     width_here = child_inverse.shape[1]
@@ -17,7 +24,7 @@
     masked = coupling[0] * row_mask[:, None]
     gathered = lax.all_gather(masked, "row", axis=0, tiled=True)
     product = jnp.dot(
-        lax.all_gather(sigma_top, "sub", axis=1, tiled=True),
+        pass_the_spots(sigma_top, 1),
         gathered,
         precision=highest,
         preferred_element_type=jnp.float32,

time: 450 us -> 414 us (0.920)
  waiting for transfers between devices: 247 us -> 27.3 us
  blocking collectives: 68.1 us -> 285 us
  matrix products: 105 us -> 63.6 us
  local copies, waits for them, and re-layouts: 9.55 us -> 16.9 us
    all_to_all x0 -> x1, blocking collectives: none -> 216 us  [pass_the_spots(): jax.lax.all_to_all(jnp.stack(jax.lax.axis_size('sub') * [local_x]), 'sub'...]
    all_gather x1 -> x0, waiting for transfers between devices: 124 us -> none  [local(): lax.all_gather(sigma_top, 'sub', axis=1, tiled=True)]
    all_gather x1, waiting for transfers between devices: 97 us -> 0.01 us  [local(): gathered = lax.all_gather(masked, 'row', axis=0, tiled=True)]
    dot_general x1, matrix products: 92.2 us -> 51 us  [local(): jnp.dot(pass_the_spots(sigma_top, 1), gathered, precision=highest, prefer...]
    another operation x0 -> x1, local copies, waits for them, and re-layouts: none -> 8.16 us  [pass_the_spots(): jnp.stack(jax.lax.axis_size('sub') * [local_x])]
  transfers between devices with their start and end apart: 3 -> 2, of which waited for: 3 -> 1; matrix products, arithmetic and copies ran while one was open for 1% -> 3% of each run, Pallas kernels for 0% -> 0%
where the time goes in v1:
time: 414 us
  blocking collectives  285 us (69%)
  matrix products  63.6 us (15%)
  waiting for transfers between devices  27.3 us (7%)
  local copies, waits for them, and re-layouts  16.9 us (4%)
  between operations  14.1 us (3%)
  other arithmetic  7.16 us (2%)
    all_to_all x1, blocking collectives, pass_the_spots(): jax.lax.all_to_all(jnp.stack(jax.lax.axis_size('sub') * [local_x]), 'sub'...  216 us
    unnamed x1, blocking collectives  68.1 us
    dot_general x1, matrix products, local(): jnp.dot(pass_the_spots(sigma_top, 1), gathered, precision=highest, prefer...  51 us
    reduce_scatter x1, waiting for transfers between devices, local(): lax.psum_scatter(lax.dot_general(masked, sep_part, (((0,), (0,)), ((), ()...  27.3 us
    dot_general x1, matrix products, local(): lax.dot_general(masked, sep_part, (((0,), (0,)), ((), ())), precision=hig...  12.5 us
  transfers between devices with their start and end apart: 2, of which 1 were waited for; matrix products, arithmetic and copies ran while one was open for 3% of the time, Pallas kernels for 0%

profile of v1, /device:TPU:1, one launch (start us, length us, event | category | flops | bytes accessed | tf_op | source)
XLA Modules:
  0.0 413.7 jit_solution(2380655108738818690)
XLA Ops:
  7.2 0.0 all-gather.2.cloned.1.call-start
  7.2 0.7 convert_bitcast_fusion
  7.9 0.1 broadcast_in_dim.17
  8.0 3.3 bitcast_multiply_fusion
  11.3 0.0 all-gather.2.cloned.1.call-update
  11.3 0.0 reduce-scatter.2.cloned.1.call-start
  11.4 1.2 copy-done.1
  12.6 0.4 copy.10
  13.0 8.2 %stack.2 = f32[16,768,384]{1,2,0:T(8,128)} broadcast(f32[768,384]{0,1:T(8,128)S(1)} %copy.10), dimensions={1,2} | broadcast | bytes 20054016 | tf_op jit(solution)/shard_map/stack | solution.py:13
  21.1 216.5 %all_to_all.5 = f32[16,768,384]{1,2,0:T(8,128)} all-to-all(f32[16,768,384]{1,2,0:T(8,128)} %stack.2), channel_id=1, replica_groups=mesh['sub'=16,'row'=8] {'sub'}, dimensions={0} | all-to-all | bytes 37748736 | tf_op jit(solution)/shard_map/all_to_all | solution.py:13
  237.6 51.0 %fusion.2 = f32[768,768]{1,0:T(8,128)S(1)} fusion(f32[6144,768]{1,0:T(8,128)} %all-gather.2.cloned.1.call-done, f32[768,6144]{0,1:T(8,128)} %bitcast.19), kind=kOutput, calls=%fused_computation.12 | convolution fusion | flops 43486543872 | bytes 40108032 | tf_op jit(solution)/shard_map/dot_general | solution.py:26
  288.7 12.5 %fusion = f32[768,768]{1,0:T(8,128)} fusion(f32[768,768]{1,0:T(8,128)S(1)} %copy-done, f32[768,768]{1,0:T(8,128)S(1)} %fusion.2), kind=kOutput, calls=%fused_computation.3 | convolution fusion | flops 5436407808 | bytes 7077888 | tf_op jit(solution)/shard_map/dot_general | solution.py:34
  301.2 0.0 reduce-scatter.2.cloned.1.call-update
  301.2 0.6 copy-done.5
  301.9 1.6 negate_bitcast_fusion
  303.5 3.1 copy.11
  306.5 27.3 %reduce-scatter.2.cloned.1.call-done = f32[96,768]{1,0:T(8,128)} async-done(((f32[768,768]{1,0:T(8,128)}), f32[96,768]{1,0:T(8,128)}) %reduce-scatter.2.cloned.1.call-update) | async-done | bytes 294928 | tf_op jit(solution)/shard_map/reduce_scatter | solution.py:33
  333.8 1.0 bitcast_subtract_fusion
  334.8 0.1 constant_dynamic-slice_fusion
  334.9 1.2 gather_fusion
  336.2 0.3 dynamic-update-slice
  336.5 68.1 %all-reduce = f32[12288]{0:T(1024)S(1)} all-reduce(f32[12288]{0:T(1024)S(1)} %dynamic-update-slice), channel_id=1, replica_groups=mesh['sub'=16,'row'=8] {'sub','row'}, use_global_device_ids=true, to_apply=%add | all-reduce | flops 12288 | bytes 98304
  404.5 1.7 gather_fusion.1
  406.3 0.6 add.25
  (16 shorter events, 0.1 us)
Async XLA Ops:
  7.2 230.4 %all-gather.2.cloned.1.call-start = ((), (), s32[]{:S(2)}) async-start(), calls=%async_computation.2 | async-start | bytes 21233664 | tf_op jit(solution)/shard_map/all_gather | solution.py:25
  11.3 1.3 copy-start.1
  11.3 322.5 %reduce-scatter.2.cloned.1.call-start = ((), (), s32[]{:S(2)}) async-start(), calls=%async_computation.3 | async-start | bytes 2654208 | tf_op jit(solution)/shard_map/reduce_scatter | solution.py:33
  237.6 51.1 %copy-start = (f32[768,768]{1,0:T(8,128)S(1)}, f32[768,768]{1,0:T(8,128)}, u32[]{:S(2)}) copy-start(f32[768,768]{1,0:T(8,128)} %bitcast_multiply_fusion) | copy-start | bytes 7077892
  301.2 0.7 copy-start.5
  303.5 30.4 %copy-start.3 = (f32[1,96,768]{2,1,0:T(8,128)S(1)}, f32[1,96,768]{2,1,0:T(8,128)}, u32[]{:S(2)}) copy-start(f32[1,96,768]{2,1,0:T(8,128)} %param.8) | copy-start | bytes 884740
  306.5 99.7 %copy-start.4 = (f32[256]{0:T(256)S(1)}, f32[256]{0:T(256)}, u32[]{:S(2)}) copy-start(f32[256]{0:T(256)} %param.11) | copy-start | bytes 3076
  334.8 72.0 %copy-start.2 = (f32[96,768]{1,0:T(8,128)}, f32[96,768]{1,0:T(8,128)S(1)}, u32[]{:S(2)}) copy-start(f32[96,768]{1,0:T(8,128)S(1)} %bitcast_subtract_fusion) | copy-start | bytes 884740
Sparse Core Ops, SparseCore 0:
  11.5 97.6 all-gather.1
  301.3 32.4 reduce-scatter.1
